TPU v7x, 256 devices: a whole 4x4x8 slice. The times are simulated.
256 devices in a mesh: noise: 8 (over x, y_hi), row: 4 (over y_lo, core), col: 8 (over z).
Axes of the slice: x: 4, y: 4 (y_hi: 2, y_lo: 2; y = y_hi * 2 + y_lo), z: 8, core: 2. Of those that a mesh axis runs over, the one named last changes fastest.
Arguments:
- image: bfloat16 [1024, 256, 128], P(('noise', 'row'), 'col'), parts along dimension 0, may hold values from -6 to 6
- noise_level: int32 [8], P('noise'), parts along dimension 0, may hold values from 0 to 7
- cond_table: float32 [8, 256], replicated, may hold values from -6 to 6
- ada_fine: float32 [256, 128], replicated, may hold values from -0.375 to 0.375
- fine_qkv: bfloat16 [128, 384], replicated, may hold values from -0.5 to 0.5
- fine_scale: float32 [2], replicated, may hold values from 4 to 16
- fine_out_w: bfloat16 [128, 128], replicated, may hold values from -0.5 to 0.5
- fine_post: float32 [128], replicated, may hold values from 0.1 to 1.9
- merge_w: bfloat16 [512, 256], replicated, may hold values from -0.25 to 0.25
- coarse_in_w: bfloat16 [256, 1024], replicated, may hold values from -0.375 to 0.375
- ada_coarse: float32 [256, 1024], replicated, may hold values from -0.375 to 0.375
- coarse_qkv: bfloat16 [3, 1024, 1024], P(None, None, 'col'), may hold values from -0.1875 to 0.1875
- coarse_scale: float32 [16], P('col'), may hold values from 4 to 16
- coarse_out_w: bfloat16 [1024, 1024], P('col'), may hold values from -0.1875 to 0.1875
- coarse_post: float32 [1024], replicated, may hold values from 0.1 to 1.9
Outputs:
- fine_out: bfloat16 [1024, 256, 128], P(('noise', 'row'), 'col'), parts along dimension 0
- coarse_out: bfloat16 [64, 16, 1024], P(('noise', 'row'), 'col'), parts along dimension 0
There are 8 independent parts, one for each index of `noise`. A program takes and returns all parts, laid end to end along the dimension named above; an argument that names none is the same for every part. Nothing has to cross between parts.
All inputs are finite; a program needn't handle non-finite values.
Results may differ from a plain program's by a relative error of at most 0.035.
Values may be sent and summed in bfloat16 or wider, within the bound.
No kernel may reach another device: no remote copies, remote signals or barrier semaphores. Data moves between devices by JAX's collectives and lax.ppermute only.
A program may use at most 128 MiB of HBM per device.

v0:
```python
import jax
import jax.numpy as jnp
from jax import lax
from jax.sharding import PartitionSpec as P

HEAD = 64
TILE = 32
POOL = 8


def with_halo(x, sides, width):
    for axis, dim in sides:
        devices, length = (lax.axis_size(axis), x.shape[dim])
        up = [(i, (i + 1) % devices) for i in range(devices - 1)]
        down = [(j, i) for i, j in up]
        last = lax.slice_in_dim(x, length - width, length, axis=dim)
        initial = lax.slice_in_dim(x, 0, width, axis=dim)
        before = lax.ppermute(last, axis, up)
        after = lax.ppermute(initial, axis, down)
        x = jnp.concatenate([before, x, after], axis=dim)
    return x


def rms(value):
    return value * lax.rsqrt(jnp.mean(value * value, axis=-1, keepdims=True) + 1e-06)


def cosine(value, heads):
    shaped = value.reshape(value.shape[:-1] + (heads, HEAD))
    return rms(shaped).reshape(value.shape)


def attend(queries, keys, values, valid, scale, heads):
    results = []
    for head in range(heads):
        low = head * HEAD
        scores = jnp.dot(
            queries[:, low : low + HEAD],
            keys[:, low : low + HEAD].T,
            preferred_element_type=jnp.float32,
        )
        scores = scores * (scale[head] / HEAD)
        if valid is not None:
            scores = jnp.where(valid[None, :], scores, -jnp.inf)
        top = jnp.max(scores, axis=-1, keepdims=True)
        expo = jnp.exp(scores - top)
        if valid is not None:
            expo = jnp.where(valid[None, :], expo, 0.0)
        weights = (expo / jnp.sum(expo, axis=-1, keepdims=True)).astype(jnp.bfloat16)
        results.append(
            jnp.dot(weights, values[:, low : low + HEAD], preferred_element_type=jnp.float32)
        )
    return jnp.concatenate(results, axis=-1).astype(jnp.bfloat16)


def attend_blocks(queries, keys, values, valid, scale, heads):
    count, width = queries.shape
    block = min(512, count)
    grouped = queries.reshape(count // block, block, width)

    def one_block(part_q):
        return attend(part_q, keys, values, valid, scale, heads)

    return lax.map(one_block, grouped).reshape(count, width)


def body(
    image,
    noise_level,
    cond_table,
    ada_fine,
    fine_qkv,
    fine_scale,
    fine_out_w,
    fine_post,
    merge_w,
    coarse_in_w,
    ada_coarse,
    coarse_qkv,
    coarse_scale,
    coarse_out_w,
    coarse_post,
):
    highest = lax.Precision.HIGHEST
    tile = TILE
    rows_loc, cols_loc, width = image.shape
    heads = width // HEAD
    levels = jnp.arange(cond_table.shape[0], dtype=jnp.int32)
    hot = (levels == noise_level[0]).astype(jnp.float32)
    cond = jnp.dot(hot, cond_table, precision=highest)
    fine_gain = 1.0 + jnp.dot(cond, ada_fine, precision=highest)
    coarse_gain = 1.0 + jnp.dot(cond, ada_coarse, precision=highest)
    xfull = image.astype(jnp.float32)
    xn = (rms(xfull) * fine_gain).astype(jnp.bfloat16)
    qproj = jnp.dot(xn.reshape(-1, width), fine_qkv[:, :width], preferred_element_type=jnp.float32)
    queries = cosine(qproj, heads).astype(jnp.bfloat16).reshape(rows_loc, cols_loc, width)
    shape = xn.shape[:2]
    proj = jnp.dot(xn.reshape(-1, width), fine_qkv[:, width:], preferred_element_type=jnp.float32)
    proj = proj.reshape(shape + (2 * width,))
    keys_out = cosine(proj[..., :width], heads).astype(jnp.bfloat16)
    values_out = proj[..., width:].astype(jnp.bfloat16)
    both = jnp.stack([keys_out, values_out], axis=0)
    padded = with_halo(both, (("row", 1), ("col", 2)), tile)
    keys_pad = padded[0]
    values_pad = padded[1]
    grid_rows = rows_loc * lax.axis_size("row")
    grid_cols = cols_loc * lax.axis_size("col")
    row_ids = (
        lax.axis_index("row") * rows_loc - tile + jnp.arange(rows_loc + 2 * tile, dtype=jnp.int32)
    )
    col_ids = (
        lax.axis_index("col") * cols_loc - tile + jnp.arange(cols_loc + 2 * tile, dtype=jnp.int32)
    )
    row_ok = (row_ids >= 0) & (row_ids < grid_rows)
    col_ok = (col_ids >= 0) & (col_ids < grid_cols)
    q_tile = queries.reshape(tile * tile, width)
    k_win = keys_pad.reshape(-1, width)
    v_win = values_pad.reshape(-1, width)
    valid = (row_ok[:, None] & col_ok[None, 0 : 3 * tile]).reshape(-1)
    result = attend_blocks(q_tile, k_win, v_win, valid, fine_scale, heads)
    pieces = [result.reshape(tile, tile, width)]
    attended = jnp.concatenate(pieces, axis=1)
    branch = jnp.dot(attended.reshape(-1, width), fine_out_w, preferred_element_type=jnp.float32)
    branch = branch.reshape(rows_loc, cols_loc, width)
    fine_out = (xfull + rms(branch) * fine_post).astype(jnp.bfloat16)
    merge_width = merge_w.shape[1]
    blocks = (
        fine_out.reshape(rows_loc // 2, 2, cols_loc // 2, 2, width)
        .transpose(0, 2, 1, 3, 4)
        .reshape(-1, 4 * width)
    )
    merged = jnp.dot(blocks, merge_w, preferred_element_type=jnp.float32).astype(jnp.bfloat16)
    pool_rows = rows_loc // (2 * POOL)
    pool_cols = cols_loc // (2 * POOL)
    merged = merged.reshape(pool_rows, POOL, pool_cols, POOL, merge_width).astype(jnp.float32)
    pooled = jnp.mean(merged, axis=(1, 3)).astype(jnp.bfloat16).reshape(-1, merge_width)
    coarse_in = jnp.dot(pooled, coarse_in_w, preferred_element_type=jnp.float32)
    cn = (rms(coarse_in) * coarse_gain).astype(jnp.bfloat16)
    coarse_width = cn.shape[1]
    local_width = coarse_qkv.shape[2]
    local_heads = local_width // HEAD
    proj = jnp.einsum(
        "nd,kde->kne",
        lax.all_gather(cn, ("row", "col"), axis=0, tiled=True),
        coarse_qkv,
        preferred_element_type=jnp.float32,
    )
    q_part = cosine(proj[0], local_heads)
    k_part = cosine(proj[1], local_heads)
    projected = jnp.concatenate([q_part, k_part, proj[2]], axis=-1).astype(jnp.bfloat16)
    own_count = cn.shape[0]
    row_count = own_count * lax.axis_size("col")
    row_start = lax.axis_index("row") * row_count
    q_rows = lax.dynamic_slice_in_dim(projected[:, :local_width], row_start, row_count, 0)
    k_all = projected[:, local_width : 2 * local_width]
    v_all = projected[:, 2 * local_width :]
    coarse_attended = attend(q_rows, k_all, v_all, None, coarse_scale, local_heads)
    coarse_branch = lax.psum_scatter(
        jnp.dot(coarse_attended, coarse_out_w, preferred_element_type=jnp.float32).astype(
            jnp.bfloat16
        ),
        "col",
        scatter_dimension=0,
        tiled=True,
    ).astype(jnp.float32)
    coarse_out = (coarse_in + rms(coarse_branch) * coarse_post).astype(jnp.bfloat16)
    coarse_out = coarse_out.reshape(pool_rows, pool_cols, coarse_width)
    return (fine_out, coarse_out)


def solution(mesh):
    in_specs = (
        P(("noise", "row"), "col", None),
        P("noise"),
        P(),
        P(),
        P(),
        P(),
        P(),
        P(),
        P(),
        P(),
        P(),
        P(None, None, "col"),
        P("col"),
        P("col", None),
        P(),
    )
    out_specs = (P(("noise", "row"), "col", None), P(("noise", "row"), "col", None))
    return jax.shard_map(body, mesh=mesh, in_specs=in_specs, out_specs=out_specs, check_vma=False)
```

profile of v0, /device:TPU:2, one launch (start us, length us, event | category | flops | bytes accessed | tf_op | source)
XLA Modules:
  0.0 353.1 jit_solution(10420121565007312929)
XLA Ops:
  16.0 1.9 reduce_sum.123
  20.3 2.2 mul.197
  25.1 1.8 collective-permute-start
  28.4 3.6 %collective-permute-done.1 = bf16[2,32,32,128]{3,2,1,0:T(8,128)(2,1)S(1)} collective-permute-done((bf16[2,32,32,128]{3,2,1,0:T(8,128)(2,1)S(1)}, bf16[2,32,32,128]{3,2,1,0:T(8,128)(2,1)S(1)}, u32[]{:S(2)}, u32[]{:S(2)}) %collective-permute-start.1) | collective-permute-done | bytes 524320 | tf_op jit(solution)/shard_map/ppermute | solution.py:19
  33.3 5.0 %collective-permute-start.2 = (bf16[2,96,32,128]{3,2,1,0:T(8,128)(2,1)}, bf16[2,96,32,128]{3,2,1,0:T(8,128)(2,1)}, u32[]{:S(2)}, u32[]{:S(2)}) collective-permute-start(bf16[2,96,32,128]{3,2,1,0:T(8,128)(2,1)} %pad_maximum_fusion.2), channel_id=1, source_target_pairs={{0,1},{1,2},{2,3},{3,4},{4,5},{5,6},{6,7},{8,9},{9,10},{10,11},{11... | collective-permute-start | bytes 4718600 | tf_op jit(solution)/shard_map/ppermute | solution.py:18
  44.7 2.3 copy.42
  50.1 15.4 %collective-permute-done.2 = bf16[2,96,32,128]{3,2,1,0:T(8,128)(2,1)} collective-permute-done((bf16[2,96,32,128]{3,2,1,0:T(8,128)(2,1)}, bf16[2,96,32,128]{3,2,1,0:T(8,128)(2,1)}, u32[]{:S(2)}, u32[]{:S(2)}) %collective-permute-start.2) | collective-permute-done | bytes 1572896 | tf_op jit(solution)/shard_map/ppermute | solution.py:18
  65.6 5.8 %collective-permute-done.3 = bf16[2,96,32,128]{3,2,1,0:T(8,128)(2,1)} collective-permute-done((bf16[2,96,32,128]{3,2,1,0:T(8,128)(2,1)}, bf16[2,96,32,128]{3,2,1,0:T(8,128)(2,1)}, u32[]{:S(2)}, u32[]{:S(2)}) %collective-permute-start.3) | collective-permute-done | bytes 1572896 | tf_op jit(solution)/shard_map/ppermute | solution.py:19
  71.4 8.8 %pad_maximum_fusion.1 = bf16[2,96,96,128]{3,2,1,0:T(8,128)(2,1)S(1)} fusion(bf16[2,96,32,128]{3,2,1,0:T(8,128)(2,1)} %collective-permute-done.3, bf16[2,32,32,128]{3,2,1,0:T(8,128)(2,1)S(1)} %collective-permute-done.1, bf16[1,32,32,128]{3,2,1,0:T(8,128)(2,1)S(1)} %fusion.38, bf16[1,32,32,128]{3,2,1,0:T(8,128)(2,1)S(1)} %fusion.37, ...), kind=kLoop, calls=%fused_computation.33 | loop fusion | flops 28311552 | bytes 9437184 | tf_op jit(solution)/shard_map/concatenate | solution.py:20
  80.2 2.2 fusion.72
  82.5 118.6 %while.13 = (s32[]{:T(128)}, bf16[2,512,128]{2,1,0:T(8,128)(2,1)}, bf16[2,512,128]{2,1,0:T(8,128)(2,1)S(1)}, bf16[9216,128]{1,0:T(8,128)(2,1)S(1)}, f32[]{:T(128...) while((s32[]{:T(128)}, bf16[2,512,128]{2,1,0:T(8,128)(2,1)}, ...), condition=%wide.region_8.9_spmd.clone, body=%wide.region_3.8_spmd.clone.sunk | while | flops 2548374528 | bytes 133657432 | solution.py:64
  82.9 7.8 %fusion.104 = (f32[512]{0:T(512)S(1)}, f32[512,9216]{1,0:T(8,128)}) fusion(f32[]{:T(128)} %get-tuple-element.291, pred[9216]{0:T(1024)(128)(4,1)S(1)} %broadcast_in_dim.143, bf16[9216,128]{1,0:T(8,128)(2,1)S(1)} %get-tuple-element.290, bf16[512,128]{1,0:T(8,128)(2,1)S(1)} %dynamic-slice_bitcast_fusion.2), kind=kOutput, calls=%fused_computation.7.clone.1 | convolution fusion | flops 618135040 | bytes 21376004 | tf_op jit(solution)/shard_map/while/body/eval_jaxpr/dot_general | solution.py:37
  90.7 18.1 %fusion.105 = (f32[512]{0:T(512)S(1)}, f32[512]{0:T(512)S(1)}, f32[512,9216]{1,0:T(8,128)}) fusion(f32[512,9216]{1,0:T(8,128)} %get-tuple-element.262, f32[512]{0:T(512)S(1)} %get-tuple-element.263, f32[]{:T(128)} %get-tuple-element.291, pred[9216]{0:T(1024)(128)(4,1)S(1)} %broadcast_in_dim.143, f32[]{:T(128)} %get-tuple-element.293, ...), kind=kOutput, calls=%fused_computation.9.clone.1 | convolution fusion | flops 641727488 | bytes 40254472 | tf_op jit(solution)/shard_map/while/body/eval_jaxpr/dot_general | solution.py:37
  108.9 9.4 %fusion.108 = bf16[1,512,64]{1,2,0:T(8,128)(2,1)S(1)} fusion(bf16[9216,128]{1,0:T(8,128)(2,1)S(1)} %copy-done.4, f32[512,9216]{1,0:T(8,128)} %get-tuple-element.262, f32[512]{0:T(512)S(1)} %get-tuple-element.266, f32[512]{0:T(512)S(1)} %get-tuple-element.263, f32[]{:T(128)} %get-tuple-element.291, pred[9216]{0:T(1024)(128)(4,1)S(1)} %broadcast_in_dim.143), kind=kOutput, calls=%fused_computation.21.clone.1 | convolution fusion | flops 632324096 | bytes 21312516 | tf_op jit(solution)/shard_map/while/body/eval_jaxpr/dot_general | solution.py:51
  118.3 11.7 %fusion.106 = f32[512]{0:T(512)S(1)} fusion(f32[512,9216]{1,0:T(8,128)} %get-tuple-element.264, f32[512]{0:T(512)S(1)} %get-tuple-element.265, f32[]{:T(128)} %get-tuple-element.293, pred[9216]{0:T(1024)(128)(4,1)S(1)} %broadcast_in_dim.143), kind=kLoop, calls=%fused_computation.10.clone.1 | loop fusion | flops 23592448 | bytes 18887684 | tf_op jit(solution)/shard_map/while/body/eval_jaxpr/reduce_sum | solution.py:49
  130.0 11.1 %fusion.107 = bf16[1,512,64]{1,2,0:T(8,128)(2,1)S(1)} fusion(bf16[9216,128]{1,0:T(8,128)(2,1)} %get-tuple-element.292, f32[512,9216]{1,0:T(8,128)} %get-tuple-element.264, f32[512]{0:T(512)S(1)} %fusion.106, f32[512]{0:T(512)S(1)} %get-tuple-element.265, f32[]{:T(128)} %get-tuple-element.293, pred[9216]{0:T(1024)(128)(4,1)S(1)} %broadcast_in_dim.143), kind=kOutput, calls=%fused_computation.22.clone.1 | convolution fusion | flops 632324096 | bytes 21312516 | tf_op jit(solution)/shard_map/while/body/eval_jaxpr/dot_general | solution.py:51
  142.1 7.8 %fusion.104 = (f32[512]{0:T(512)S(1)}, f32[512,9216]{1,0:T(8,128)}) fusion(f32[]{:T(128)} %get-tuple-element.291, pred[9216]{0:T(1024)(128)(4,1)S(1)} %broadcast_in_dim.143, bf16[9216,128]{1,0:T(8,128)(2,1)S(1)} %get-tuple-element.290, bf16[512,128]{1,0:T(8,128)(2,1)S(1)} %dynamic-slice_bitcast_fusion.2), kind=kOutput, calls=%fused_computation.7.clone.1 | convolution fusion | flops 618135040 | bytes 21376004 | tf_op jit(solution)/shard_map/while/body/eval_jaxpr/dot_general | solution.py:37
  149.9 18.1 %fusion.105 = (f32[512]{0:T(512)S(1)}, f32[512]{0:T(512)S(1)}, f32[512,9216]{1,0:T(8,128)}) fusion(f32[512,9216]{1,0:T(8,128)} %get-tuple-element.262, f32[512]{0:T(512)S(1)} %get-tuple-element.263, f32[]{:T(128)} %get-tuple-element.291, pred[9216]{0:T(1024)(128)(4,1)S(1)} %broadcast_in_dim.143, f32[]{:T(128)} %get-tuple-element.293, ...), kind=kOutput, calls=%fused_computation.9.clone.1 | convolution fusion | flops 641727488 | bytes 40254472 | tf_op jit(solution)/shard_map/while/body/eval_jaxpr/dot_general | solution.py:37
  168.1 9.4 %fusion.108 = bf16[1,512,64]{1,2,0:T(8,128)(2,1)S(1)} fusion(bf16[9216,128]{1,0:T(8,128)(2,1)S(1)} %copy-done.4, f32[512,9216]{1,0:T(8,128)} %get-tuple-element.262, f32[512]{0:T(512)S(1)} %get-tuple-element.266, f32[512]{0:T(512)S(1)} %get-tuple-element.263, f32[]{:T(128)} %get-tuple-element.291, pred[9216]{0:T(1024)(128)(4,1)S(1)} %broadcast_in_dim.143), kind=kOutput, calls=%fused_computation.21.clone.1 | convolution fusion | flops 632324096 | bytes 21312516 | tf_op jit(solution)/shard_map/while/body/eval_jaxpr/dot_general | solution.py:51
  177.5 11.7 %fusion.106 = f32[512]{0:T(512)S(1)} fusion(f32[512,9216]{1,0:T(8,128)} %get-tuple-element.264, f32[512]{0:T(512)S(1)} %get-tuple-element.265, f32[]{:T(128)} %get-tuple-element.293, pred[9216]{0:T(1024)(128)(4,1)S(1)} %broadcast_in_dim.143), kind=kLoop, calls=%fused_computation.10.clone.1 | loop fusion | flops 23592448 | bytes 18887684 | tf_op jit(solution)/shard_map/while/body/eval_jaxpr/reduce_sum | solution.py:49
  189.2 11.1 %fusion.107 = bf16[1,512,64]{1,2,0:T(8,128)(2,1)S(1)} fusion(bf16[9216,128]{1,0:T(8,128)(2,1)} %get-tuple-element.292, f32[512,9216]{1,0:T(8,128)} %get-tuple-element.264, f32[512]{0:T(512)S(1)} %fusion.106, f32[512]{0:T(512)S(1)} %get-tuple-element.265, f32[]{:T(128)} %get-tuple-element.293, pred[9216]{0:T(1024)(128)(4,1)S(1)} %broadcast_in_dim.143), kind=kOutput, calls=%fused_computation.22.clone.1 | convolution fusion | flops 632324096 | bytes 21312516 | tf_op jit(solution)/shard_map/while/body/eval_jaxpr/dot_general | solution.py:51
  206.7 57.0 %all-gather = bf16[32,4,1024]{2,1,0:T(4,128)(2,1)S(1)} all-gather(bf16[1,4,1024]{2,1,0:T(4,128)(2,1)S(1)} %fusion.59), channel_id=1, replica_groups=mesh['noise'=8,'row'=4,'col'=8] {'row','col'}, dimensions={0}, use_global_device_ids=true | all-gather | bytes 270336 | tf_op jit(solution)/shard_map/all_gather | solution.py:144
  266.9 1.8 convolution_convert_fusion.1
  270.0 74.0 %all-reduce.3.cloned.1.call-done = bf16[32,1024]{1,0:T(8,128)(2,1)} async-done(((bf16[32,1024]{1,0:T(8,128)(2,1)}), bf16[32,1024]{1,0:T(8,128)(2,1)}) %all-reduce.3.cloned.1.call-update) | async-done | bytes 65552
  (108 shorter events, 36.2 us)
Async XLA Ops:
  7.2 41.8 %copy-start = (f32[256,1024]{1,0:T(8,128)S(1)}, f32[256,1024]{1,0:T(8,128)}, u32[]{:S(2)}) copy-start(f32[256,1024]{1,0:T(8,128)} %param.27) | copy-start | bytes 3145732
  7.2 336.8 %all-reduce.3.cloned.1.call-start = ((), (), s32[]{:S(2)}) async-start(), calls=%async_computation | async-start | bytes 131072
  12.2 2.1 copy-start.3
  12.2 30.6 %copy-start.9 = (f32[2]{0:T(128)S(1)}, f32[2]{0:T(128)}, u32[]{:S(2)}) copy-start(f32[2]{0:T(128)} %param.22) | copy-start | bytes 28
  13.4 33.6 %copy-start.10 = (f32[2]{0:T(128)S(1)}, f32[2]{0:T(128)}, u32[]{:S(2)}) copy-start(f32[2]{0:T(128)} %param.29) | copy-start | bytes 28
  25.1 3.3 collective-permute-start
  26.9 5.1 %collective-permute-start.1 = (bf16[2,32,32,128]{3,2,1,0:T(8,128)(2,1)S(1)}, bf16[2,32,32,128]{3,2,1,0:T(8,128)(2,1)S(1)}, u32[]{:S(2)}, u32[]{:S(2)}) collective-permute-start(bf16[2,32,32,128]{3,2,1,0:T(8,128)(2,1)S(1)} %pad_maximum_fusion.3), channel_id=1, source_target_pairs={{8,0},{16,8},{24,16},{9,1},{17,9},{25,17},{10,2},{18,10},{26,18},{... | collective-permute-start | bytes 1572872 | tf_op jit(solution)/shard_map/ppermute | solution.py:19
  33.3 32.2 %collective-permute-start.2 = (bf16[2,96,32,128]{3,2,1,0:T(8,128)(2,1)}, bf16[2,96,32,128]{3,2,1,0:T(8,128)(2,1)}, u32[]{:S(2)}, u32[]{:S(2)}) collective-permute-start(bf16[2,96,32,128]{3,2,1,0:T(8,128)(2,1)} %pad_maximum_fusion.2), channel_id=1, source_target_pairs={{0,1},{1,2},{2,3},{3,4},{4,5},{5,6},{6,7},{8,9},{9,10},{10,11},{11... | collective-permute-start | bytes 4718600 | tf_op jit(solution)/shard_map/ppermute | solution.py:18
  38.3 33.1 %collective-permute-start.3 = (bf16[2,96,32,128]{3,2,1,0:T(8,128)(2,1)}, bf16[2,96,32,128]{3,2,1,0:T(8,128)(2,1)}, u32[]{:S(2)}, u32[]{:S(2)}) collective-permute-start(bf16[2,96,32,128]{3,2,1,0:T(8,128)(2,1)} %pad_maximum_fusion.2), channel_id=1, source_target_pairs={{1,0},{2,1},{3,2},{4,3},{5,4},{6,5},{7,6},{9,8},{10,9},{11,10},{12... | collective-permute-start | bytes 4718600 | tf_op jit(solution)/shard_map/ppermute | solution.py:19
  50.1 32.3 %copy-start.2 = (bf16[2,512,128]{2,1,0:T(8,128)(2,1)S(1)}, bf16[2,512,128]{2,1,0:T(8,128)(2,1)}, u32[]{:S(2)}) copy-start(bf16[2,512,128]{2,1,0:T(8,128)(2,1)} %copy.39) | copy-start | bytes 786436
  82.4 118.7 %copy-start.6 = (bf16[128,128]{1,0:T(8,128)(2,1)S(1)}, bf16[128,128]{1,0:T(8,128)(2,1)}, u32[]{:S(2)}) copy-start(bf16[128,128]{1,0:T(8,128)(2,1)} %param.23) | copy-start | bytes 98308
  82.4 120.1 %copy-start.11 = (f32[128]{0:T(128)S(1)}, f32[128]{0:T(128)}, u32[]{:S(2)}) copy-start(f32[128]{0:T(128)} %param.24) | copy-start | bytes 1540
  82.4 124.2 %copy-start.7 = (f32[1024]{0:T(1024)S(1)}, f32[1024]{0:T(1024)}, u32[]{:S(2)}) copy-start(f32[1024]{0:T(1024)} %broadcast_add_fusion) | copy-start | bytes 12292
  82.4 186.3 %copy-start.12 = (u32[256]{0:T(256)S(1)}, u32[256]{0:T(256)}, u32[]{:S(2)}) copy-start(u32[256]{0:T(256)} %constant.97) | copy-start | bytes 3076
  82.5 262.4 %copy-start.8 = (f32[1024]{0:T(1024)S(1)}, f32[1024]{0:T(1024)}, u32[]{:S(2)}) copy-start(f32[1024]{0:T(1024)} %param.31) | copy-start | bytes 12292
  90.7 18.1 %copy-start.4 = (bf16[9216,128]{1,0:T(8,128)(2,1)S(1)}, bf16[9216,128]{1,0:T(8,128)(2,1)}, u32[]{:S(2)}) copy-start(bf16[9216,128]{1,0:T(8,128)(2,1)} %get-tuple-element.292) | copy-start | bytes 7077892 | tf_op jit(solution)/shard_map/while
  149.9 18.1 %copy-start.4 = (bf16[9216,128]{1,0:T(8,128)(2,1)S(1)}, bf16[9216,128]{1,0:T(8,128)(2,1)}, u32[]{:S(2)}) copy-start(bf16[9216,128]{1,0:T(8,128)(2,1)} %get-tuple-element.292) | copy-start | bytes 7077892 | tf_op jit(solution)/shard_map/while
  201.1 145.2 %copy-start.1 = (f32[256,1024]{1,0:T(8,128)S(1)}, f32[256,1024]{1,0:T(8,128)}, u32[]{:S(2)}) copy-start(f32[256,1024]{1,0:T(8,128)} %param.27) | copy-start | bytes 3145732
  203.7 142.6 %copy-start.5 = (bf16[32,32,128]{2,1,0:T(8,128)(2,1)}, bf16[32,32,128]{2,1,0:T(8,128)(2,1)S(1)}, u32[]{:S(2)}) copy-start(bf16[32,32,128]{2,1,0:T(8,128)(2,1)S(1)} %fusion.36) | copy-start | bytes 786436
Sparse Core Ops, SparseCore 0:
  268.9 75.0 all-reduce.2
where the time goes:
time: 354 us; the launch traced here: 353 us
  matrix products  106 us (30%)
  waiting for transfers between devices  99.1 us (28%)
  blocking collectives  57 us (16%)
  other arithmetic  44.3 us (13%)
  local copies, waits for them, and re-layouts  18.8 us (5%)
  between operations  18.3 us (5%)
  starting transfers between devices  9.34 us (3%)
    unnamed x2, waiting for transfers between devices  74 us
    all_gather x1, blocking collectives, body(): lax.all_gather(cn, ('row', 'col'), axis=0, tiled=True)  57 us
    dot_general x6, matrix products, attend(): jnp.dot(queries[:, low:low + HEAD], keys[:, low:low + HEAD].T, preferred_...  52.5 us
    dot_general x6, matrix products, attend(): jnp.dot(weights, values[:, low:low + HEAD], preferred_element_type=jnp.fl...  41.3 us
    reduce_sum x4, other arithmetic, attend(): jnp.sum(expo, axis=-1, keepdims=True)  23.8 us
    ppermute x2, waiting for transfers between devices, with_halo(): before = lax.ppermute(last, axis, up)  15.6 us
    concatenate x2, other arithmetic, with_halo(): x = jnp.concatenate([before, x, after], axis=dim)  10.2 us
    ppermute x2, waiting for transfers between devices, with_halo(): after = lax.ppermute(initial, axis, down)  9.45 us
  transfers between devices with their start and end apart: 5, of which 5 were waited for; matrix products, arithmetic and copies ran while one was open for 2% of the time, Pallas kernels for 0%

commit v1 on v0

--- a/solution.py
+++ b/solution.py
@@ -141,7 +141,10 @@
     local_heads = local_width // HEAD
     proj = jnp.einsum(
         "nd,kde->kne",
-        lax.all_gather(cn, ("row", "col"), axis=0, tiled=True),
+        jnp.concatenate(
+            lax.all_to_all(jnp.stack([cn] * lax.axis_size(("row", "col"))), ("row", "col"), 0, 0),
+            axis=0,
+        ),
         coarse_qkv,
         preferred_element_type=jnp.float32,
     )

time: 354 us -> 315 us (0.89)
  blocking collectives: 57 us -> 0 us
  starting transfers between devices: 9.34 us -> 22.8 us
  waiting for transfers between devices: 99.1 us -> 105 us
    all_gather x1 -> x0, blocking collectives: 57 us -> none  [body(): lax.all_gather(cn, ('row', 'col'), axis=0, tiled=True)]
    all_to_all x0 -> x1, starting transfers between devices: none -> 13.4 us  [body(): lax.all_to_all(jnp.stack([cn] * lax.axis_size(('row', 'col'))), ('row', '...]
    all_to_all x0 -> x1, waiting for transfers between devices: none -> 8.31 us  [body(): lax.all_to_all(jnp.stack([cn] * lax.axis_size(('row', 'col'))), ('row', '...]
    unnamed x2, waiting for transfers between devices: 74 us -> 67.8 us
    ppermute x2, waiting for transfers between devices: 15.6 us -> 19.8 us  [with_halo(): before = lax.ppermute(last, axis, up)]
  transfers between devices with their start and end apart: 5 -> 6, of which waited for: 5 -> 6; matrix products, arithmetic and copies ran while one was open for 2% -> 2% of each run, Pallas kernels for 0% -> 0%
where the time goes in v1:
time: 315 us; the launch traced here: 314 us
  waiting for transfers between devices  105 us (33%)
  matrix products  104 us (33%)
  other arithmetic  44.3 us (14%)
  starting transfers between devices  22.8 us (7%)
  local copies, waits for them, and re-layouts  18.6 us (6%)
  between operations  18.4 us (6%)
    unnamed x2, waiting for transfers between devices  67.8 us
    dot_general x6, matrix products, attend(): jnp.dot(queries[:, low:low + HEAD], keys[:, low:low + HEAD].T, preferred_...  52.5 us
    dot_general x6, matrix products, attend(): jnp.dot(weights, values[:, low:low + HEAD], preferred_element_type=jnp.fl...  41.3 us
    reduce_sum x4, other arithmetic, attend(): jnp.sum(expo, axis=-1, keepdims=True)  23.8 us
    ppermute x2, waiting for transfers between devices, with_halo(): before = lax.ppermute(last, axis, up)  19.8 us
    all_to_all x1, starting transfers between devices, body(): lax.all_to_all(jnp.stack([cn] * lax.axis_size(('row', 'col'))), ('row', '...  13.4 us
    concatenate x2, other arithmetic, with_halo(): x = jnp.concatenate([before, x, after], axis=dim)  10.2 us
    ppermute x2, waiting for transfers between devices, with_halo(): after = lax.ppermute(initial, axis, down)  9.44 us
  transfers between devices with their start and end apart: 6, of which 6 were waited for; matrix products, arithmetic and copies ran while one was open for 2% of the time, Pallas kernels for 0%

profile of v1, /device:TPU:2, one launch (start us, length us, event | category | flops | bytes accessed | tf_op | source)
XLA Modules:
  0.0 313.7 jit_solution(9509830773761698276)
XLA Ops:
  14.3 1.7 mul.196
  15.9 1.9 reduce_sum.123
  20.3 2.2 mul.197
  25.1 1.8 collective-permute-start
  28.3 3.6 %collective-permute-done.1 = bf16[2,32,32,128]{3,2,1,0:T(8,128)(2,1)S(1)} collective-permute-done((bf16[2,32,32,128]{3,2,1,0:T(8,128)(2,1)S(1)}, bf16[2,32,32,128]{3,2,1,0:T(8,128)(2,1)S(1)}, u32[]{:S(2)}, u32[]{:S(2)}) %collective-permute-start.1) | collective-permute-done | bytes 524320 | tf_op jit(solution)/shard_map/ppermute | solution.py:19
  33.3 5.0 %collective-permute-start.2 = (bf16[2,96,32,128]{3,2,1,0:T(8,128)(2,1)}, bf16[2,96,32,128]{3,2,1,0:T(8,128)(2,1)}, u32[]{:S(2)}, u32[]{:S(2)}) collective-permute-start(bf16[2,96,32,128]{3,2,1,0:T(8,128)(2,1)} %pad_maximum_fusion.2), channel_id=1, source_target_pairs={{0,1},{1,2},{2,3},{3,4},{4,5},{5,6},{6,7},{8,9},{9,10},{10,11},{11... | collective-permute-start | bytes 4718600 | tf_op jit(solution)/shard_map/ppermute | solution.py:18
  45.9 19.6 %collective-permute-done.2 = bf16[2,96,32,128]{3,2,1,0:T(8,128)(2,1)} collective-permute-done((bf16[2,96,32,128]{3,2,1,0:T(8,128)(2,1)}, bf16[2,96,32,128]{3,2,1,0:T(8,128)(2,1)}, u32[]{:S(2)}, u32[]{:S(2)}) %collective-permute-start.2) | collective-permute-done | bytes 1572896 | tf_op jit(solution)/shard_map/ppermute | solution.py:18
  65.5 5.8 %collective-permute-done.3 = bf16[2,96,32,128]{3,2,1,0:T(8,128)(2,1)} collective-permute-done((bf16[2,96,32,128]{3,2,1,0:T(8,128)(2,1)}, bf16[2,96,32,128]{3,2,1,0:T(8,128)(2,1)}, u32[]{:S(2)}, u32[]{:S(2)}) %collective-permute-start.3) | collective-permute-done | bytes 1572896 | tf_op jit(solution)/shard_map/ppermute | solution.py:19
  71.3 8.8 %pad_maximum_fusion.1 = bf16[2,96,96,128]{3,2,1,0:T(8,128)(2,1)S(1)} fusion(bf16[2,96,32,128]{3,2,1,0:T(8,128)(2,1)} %collective-permute-done.3, bf16[2,32,32,128]{3,2,1,0:T(8,128)(2,1)S(1)} %collective-permute-done.1, bf16[1,32,32,128]{3,2,1,0:T(8,128)(2,1)S(1)} %fusion.38, bf16[1,32,32,128]{3,2,1,0:T(8,128)(2,1)S(1)} %fusion.37, ...), kind=kLoop, calls=%fused_computation.33 | loop fusion | flops 28311552 | bytes 9437184 | tf_op jit(solution)/shard_map/concatenate | solution.py:20
  80.2 2.2 fusion.71
  82.4 118.7 %while.13 = (s32[]{:T(128)}, bf16[2,512,128]{2,1,0:T(8,128)(2,1)}, bf16[2,512,128]{2,1,0:T(8,128)(2,1)S(1)}, bf16[9216,128]{1,0:T(8,128)(2,1)S(1)}, f32[]{:T(128...) while((s32[]{:T(128)}, bf16[2,512,128]{2,1,0:T(8,128)(2,1)}, ...), condition=%wide.region_8.9_spmd.clone, body=%wide.region_3.8_spmd.clone.sunk | while | flops 2548374528 | bytes 133657432 | solution.py:64
  82.8 7.8 %fusion.103 = (f32[512]{0:T(512)S(1)}, f32[512,9216]{1,0:T(8,128)}) fusion(f32[]{:T(128)} %get-tuple-element.291, pred[9216]{0:T(1024)(128)(4,1)S(1)} %broadcast_in_dim.143, bf16[9216,128]{1,0:T(8,128)(2,1)S(1)} %get-tuple-element.290, bf16[512,128]{1,0:T(8,128)(2,1)S(1)} %dynamic-slice_bitcast_fusion.2), kind=kOutput, calls=%fused_computation.7.clone.1 | convolution fusion | flops 618135040 | bytes 21376004 | tf_op jit(solution)/shard_map/while/body/eval_jaxpr/dot_general | solution.py:37
  90.7 18.1 %fusion.104 = (f32[512]{0:T(512)S(1)}, f32[512]{0:T(512)S(1)}, f32[512,9216]{1,0:T(8,128)}) fusion(f32[512,9216]{1,0:T(8,128)} %get-tuple-element.262, f32[512]{0:T(512)S(1)} %get-tuple-element.263, f32[]{:T(128)} %get-tuple-element.291, pred[9216]{0:T(1024)(128)(4,1)S(1)} %broadcast_in_dim.143, f32[]{:T(128)} %get-tuple-element.293, ...), kind=kOutput, calls=%fused_computation.9.clone.1 | convolution fusion | flops 641727488 | bytes 40254472 | tf_op jit(solution)/shard_map/while/body/eval_jaxpr/dot_general | solution.py:37
  108.8 9.4 %fusion.107 = bf16[1,512,64]{1,2,0:T(8,128)(2,1)S(1)} fusion(bf16[9216,128]{1,0:T(8,128)(2,1)S(1)} %copy-done.4, f32[512,9216]{1,0:T(8,128)} %get-tuple-element.262, f32[512]{0:T(512)S(1)} %get-tuple-element.266, f32[512]{0:T(512)S(1)} %get-tuple-element.263, f32[]{:T(128)} %get-tuple-element.291, pred[9216]{0:T(1024)(128)(4,1)S(1)} %broadcast_in_dim.143), kind=kOutput, calls=%fused_computation.21.clone.1 | convolution fusion | flops 632324096 | bytes 21312516 | tf_op jit(solution)/shard_map/while/body/eval_jaxpr/dot_general | solution.py:51
  118.2 11.7 %fusion.105 = f32[512]{0:T(512)S(1)} fusion(f32[512,9216]{1,0:T(8,128)} %get-tuple-element.264, f32[512]{0:T(512)S(1)} %get-tuple-element.265, f32[]{:T(128)} %get-tuple-element.293, pred[9216]{0:T(1024)(128)(4,1)S(1)} %broadcast_in_dim.143), kind=kLoop, calls=%fused_computation.10.clone.1 | loop fusion | flops 23592448 | bytes 18887684 | tf_op jit(solution)/shard_map/while/body/eval_jaxpr/reduce_sum | solution.py:49
  129.9 11.1 %fusion.106 = bf16[1,512,64]{1,2,0:T(8,128)(2,1)S(1)} fusion(bf16[9216,128]{1,0:T(8,128)(2,1)} %get-tuple-element.292, f32[512,9216]{1,0:T(8,128)} %get-tuple-element.264, f32[512]{0:T(512)S(1)} %fusion.105, f32[512]{0:T(512)S(1)} %get-tuple-element.265, f32[]{:T(128)} %get-tuple-element.293, pred[9216]{0:T(1024)(128)(4,1)S(1)} %broadcast_in_dim.143), kind=kOutput, calls=%fused_computation.22.clone.1 | convolution fusion | flops 632324096 | bytes 21312516 | tf_op jit(solution)/shard_map/while/body/eval_jaxpr/dot_general | solution.py:51
  142.0 7.8 %fusion.103 = (f32[512]{0:T(512)S(1)}, f32[512,9216]{1,0:T(8,128)}) fusion(f32[]{:T(128)} %get-tuple-element.291, pred[9216]{0:T(1024)(128)(4,1)S(1)} %broadcast_in_dim.143, bf16[9216,128]{1,0:T(8,128)(2,1)S(1)} %get-tuple-element.290, bf16[512,128]{1,0:T(8,128)(2,1)S(1)} %dynamic-slice_bitcast_fusion.2), kind=kOutput, calls=%fused_computation.7.clone.1 | convolution fusion | flops 618135040 | bytes 21376004 | tf_op jit(solution)/shard_map/while/body/eval_jaxpr/dot_general | solution.py:37
  149.9 18.1 %fusion.104 = (f32[512]{0:T(512)S(1)}, f32[512]{0:T(512)S(1)}, f32[512,9216]{1,0:T(8,128)}) fusion(f32[512,9216]{1,0:T(8,128)} %get-tuple-element.262, f32[512]{0:T(512)S(1)} %get-tuple-element.263, f32[]{:T(128)} %get-tuple-element.291, pred[9216]{0:T(1024)(128)(4,1)S(1)} %broadcast_in_dim.143, f32[]{:T(128)} %get-tuple-element.293, ...), kind=kOutput, calls=%fused_computation.9.clone.1 | convolution fusion | flops 641727488 | bytes 40254472 | tf_op jit(solution)/shard_map/while/body/eval_jaxpr/dot_general | solution.py:37
  168.0 9.4 %fusion.107 = bf16[1,512,64]{1,2,0:T(8,128)(2,1)S(1)} fusion(bf16[9216,128]{1,0:T(8,128)(2,1)S(1)} %copy-done.4, f32[512,9216]{1,0:T(8,128)} %get-tuple-element.262, f32[512]{0:T(512)S(1)} %get-tuple-element.266, f32[512]{0:T(512)S(1)} %get-tuple-element.263, f32[]{:T(128)} %get-tuple-element.291, pred[9216]{0:T(1024)(128)(4,1)S(1)} %broadcast_in_dim.143), kind=kOutput, calls=%fused_computation.21.clone.1 | convolution fusion | flops 632324096 | bytes 21312516 | tf_op jit(solution)/shard_map/while/body/eval_jaxpr/dot_general | solution.py:51
  177.4 11.7 %fusion.105 = f32[512]{0:T(512)S(1)} fusion(f32[512,9216]{1,0:T(8,128)} %get-tuple-element.264, f32[512]{0:T(512)S(1)} %get-tuple-element.265, f32[]{:T(128)} %get-tuple-element.293, pred[9216]{0:T(1024)(128)(4,1)S(1)} %broadcast_in_dim.143), kind=kLoop, calls=%fused_computation.10.clone.1 | loop fusion | flops 23592448 | bytes 18887684 | tf_op jit(solution)/shard_map/while/body/eval_jaxpr/reduce_sum | solution.py:49
  189.2 11.1 %fusion.106 = bf16[1,512,64]{1,2,0:T(8,128)(2,1)S(1)} fusion(bf16[9216,128]{1,0:T(8,128)(2,1)} %get-tuple-element.292, f32[512,9216]{1,0:T(8,128)} %get-tuple-element.264, f32[512]{0:T(512)S(1)} %fusion.105, f32[512]{0:T(512)S(1)} %get-tuple-element.265, f32[]{:T(128)} %get-tuple-element.293, pred[9216]{0:T(1024)(128)(4,1)S(1)} %broadcast_in_dim.143), kind=kOutput, calls=%fused_computation.22.clone.1 | convolution fusion | flops 632324096 | bytes 21312516 | tf_op jit(solution)/shard_map/while/body/eval_jaxpr/dot_general | solution.py:51
  207.5 13.4 %all-to-all-start = ((bf16[32,4,1024]{2,1,0:T(4,128)(2,1)}), bf16[32,4,1024]{2,1,0:T(4,128)(2,1)S(1)}, u32[]{:S(2)}, u32[]{:S(2)}) async-start(bf16[32,4,1024]{2,1,0:T(4,128)(2,1)} %stack.11), calls=%async_computation | async-start | bytes 524288 | tf_op jit(solution)/shard_map/all_to_all | solution.py:145
  224.3 8.3 %all-to-all-done = bf16[32,4,1024]{2,1,0:T(4,128)(2,1)S(1)} async-done(((bf16[32,4,1024]{2,1,0:T(4,128)(2,1)}), bf16[32,4,1024]{2,1,0:T(4,128)(2,1)S(1)}, u32[]{:S(2)}, u32[]{:S(2)}) %all-to-all-start) | async-done | bytes 262176 | tf_op jit(solution)/shard_map/all_to_all | solution.py:145
  236.7 67.8 %all-reduce.3.cloned.1.call-done = bf16[32,1024]{1,0:T(8,128)(2,1)} async-done(((bf16[32,1024]{1,0:T(8,128)(2,1)}), bf16[32,1024]{1,0:T(8,128)(2,1)}) %all-reduce.3.cloned.1.call-update) | async-done | bytes 65552
  (112 shorter events, 36.5 us)
Async XLA Ops:
  7.2 37.5 %copy-start = (f32[256,1024]{1,0:T(8,128)S(1)}, f32[256,1024]{1,0:T(8,128)}, u32[]{:S(2)}) copy-start(f32[256,1024]{1,0:T(8,128)} %param.27) | copy-start | bytes 3145732
  12.2 2.1 copy-start.3
  12.2 30.6 %copy-start.10 = (f32[2]{0:T(128)S(1)}, f32[2]{0:T(128)}, u32[]{:S(2)}) copy-start(f32[2]{0:T(128)} %param.22) | copy-start | bytes 28
  25.1 3.3 %collective-permute-start = (bf16[2,32,32,128]{3,2,1,0:T(8,128)(2,1)S(1)}, bf16[2,32,32,128]{3,2,1,0:T(8,128)(2,1)S(1)}, u32[]{:S(2)}, u32[]{:S(2)}) collective-permute-start(bf16[2,32,32,128]{3,2,1,0:T(8,128)(2,1)S(1)} %pad_maximum_fusion.3), channel_id=1, source_target_pairs={{0,8},{8,16},{16,24},{1,9},{9,17},{17,25},{2,10},{10,18},{18,26},{... | collective-permute-start | bytes 1572872 | tf_op jit(solution)/shard_map/ppermute | solution.py:18
  26.8 5.1 %collective-permute-start.1 = (bf16[2,32,32,128]{3,2,1,0:T(8,128)(2,1)S(1)}, bf16[2,32,32,128]{3,2,1,0:T(8,128)(2,1)S(1)}, u32[]{:S(2)}, u32[]{:S(2)}) collective-permute-start(bf16[2,32,32,128]{3,2,1,0:T(8,128)(2,1)S(1)} %pad_maximum_fusion.3), channel_id=1, source_target_pairs={{8,0},{16,8},{24,16},{9,1},{17,9},{25,17},{10,2},{18,10},{26,18},{... | collective-permute-start | bytes 1572872 | tf_op jit(solution)/shard_map/ppermute | solution.py:19
  33.3 32.2 %collective-permute-start.2 = (bf16[2,96,32,128]{3,2,1,0:T(8,128)(2,1)}, bf16[2,96,32,128]{3,2,1,0:T(8,128)(2,1)}, u32[]{:S(2)}, u32[]{:S(2)}) collective-permute-start(bf16[2,96,32,128]{3,2,1,0:T(8,128)(2,1)} %pad_maximum_fusion.2), channel_id=1, source_target_pairs={{0,1},{1,2},{2,3},{3,4},{4,5},{5,6},{6,7},{8,9},{9,10},{10,11},{11... | collective-permute-start | bytes 4718600 | tf_op jit(solution)/shard_map/ppermute | solution.py:18
  38.3 33.1 %collective-permute-start.3 = (bf16[2,96,32,128]{3,2,1,0:T(8,128)(2,1)}, bf16[2,96,32,128]{3,2,1,0:T(8,128)(2,1)}, u32[]{:S(2)}, u32[]{:S(2)}) collective-permute-start(bf16[2,96,32,128]{3,2,1,0:T(8,128)(2,1)} %pad_maximum_fusion.2), channel_id=1, source_target_pairs={{1,0},{2,1},{3,2},{4,3},{5,4},{6,5},{7,6},{9,8},{10,9},{11,10},{12... | collective-permute-start | bytes 4718600 | tf_op jit(solution)/shard_map/ppermute | solution.py:19
  45.9 36.5 %copy-start.2 = (bf16[2,512,128]{2,1,0:T(8,128)(2,1)S(1)}, bf16[2,512,128]{2,1,0:T(8,128)(2,1)}, u32[]{:S(2)}) copy-start(bf16[2,512,128]{2,1,0:T(8,128)(2,1)} %copy.39) | copy-start | bytes 786436
  82.4 118.7 %copy-start.7 = (bf16[128,128]{1,0:T(8,128)(2,1)S(1)}, bf16[128,128]{1,0:T(8,128)(2,1)}, u32[]{:S(2)}) copy-start(bf16[128,128]{1,0:T(8,128)(2,1)} %param.23) | copy-start | bytes 98308
  82.4 120.1 %copy-start.12 = (f32[128]{0:T(128)S(1)}, f32[128]{0:T(128)}, u32[]{:S(2)}) copy-start(f32[128]{0:T(128)} %param.24) | copy-start | bytes 1540
  82.4 124.2 %copy-start.8 = (f32[1024]{0:T(1024)S(1)}, f32[1024]{0:T(1024)}, u32[]{:S(2)}) copy-start(f32[1024]{0:T(1024)} %broadcast_add_fusion) | copy-start | bytes 12292
  82.4 140.0 %copy-start.11 = (f32[2]{0:T(128)S(1)}, f32[2]{0:T(128)}, u32[]{:S(2)}) copy-start(f32[2]{0:T(128)} %param.29) | copy-start | bytes 28
  90.6 18.1 %copy-start.4 = (bf16[9216,128]{1,0:T(8,128)(2,1)S(1)}, bf16[9216,128]{1,0:T(8,128)(2,1)}, u32[]{:S(2)}) copy-start(bf16[9216,128]{1,0:T(8,128)(2,1)} %get-tuple-element.292) | copy-start | bytes 7077892 | tf_op jit(solution)/shard_map/while
  149.9 18.2 %copy-start.4 = (bf16[9216,128]{1,0:T(8,128)(2,1)S(1)}, bf16[9216,128]{1,0:T(8,128)(2,1)}, u32[]{:S(2)}) copy-start(bf16[9216,128]{1,0:T(8,128)(2,1)} %get-tuple-element.292) | copy-start | bytes 7077892 | tf_op jit(solution)/shard_map/while
  201.1 33.6 %copy-start.6 = (bf16[128,1024]{1,0:T(8,128)(2,1)S(1)}, bf16[128,1024]{1,0:T(8,128)(2,1)}, u32[]{:S(2)}) copy-start(bf16[128,1024]{1,0:T(8,128)(2,1)} %param.30) | copy-start | bytes 786436
  201.1 34.4 %copy-start.13 = (u32[256]{0:T(256)S(1)}, u32[256]{0:T(256)}, u32[]{:S(2)}) copy-start(u32[256]{0:T(256)} %constant.97) | copy-start | bytes 3076
  201.1 104.3 %copy-start.9 = (f32[1024]{0:T(1024)S(1)}, f32[1024]{0:T(1024)}, u32[]{:S(2)}) copy-start(f32[1024]{0:T(1024)} %param.31) | copy-start | bytes 12292
  201.1 105.7 %copy-start.1 = (f32[256,1024]{1,0:T(8,128)S(1)}, f32[256,1024]{1,0:T(8,128)}, u32[]{:S(2)}) copy-start(f32[256,1024]{1,0:T(8,128)} %param.27) | copy-start | bytes 3145732
  203.7 103.1 %copy-start.5 = (bf16[32,32,128]{2,1,0:T(8,128)(2,1)}, bf16[32,32,128]{2,1,0:T(8,128)(2,1)S(1)}, u32[]{:S(2)}) copy-start(bf16[32,32,128]{2,1,0:T(8,128)(2,1)S(1)} %fusion.36) | copy-start | bytes 786436
  207.5 25.1 %all-to-all-start = ((bf16[32,4,1024]{2,1,0:T(4,128)(2,1)}), bf16[32,4,1024]{2,1,0:T(4,128)(2,1)S(1)}, u32[]{:S(2)}, u32[]{:S(2)}) async-start(bf16[32,4,1024]{2,1,0:T(4,128)(2,1)} %stack.11), calls=%async_computation | async-start | bytes 524288 | tf_op jit(solution)/shard_map/all_to_all | solution.py:145
  220.9 83.7 %all-reduce.3.cloned.1.call-start = ((), (), s32[]{:S(2)}) async-start(), calls=%async_computation.1 | async-start | bytes 131072
Sparse Core Ops, SparseCore 0:
  235.6 68.8 all-reduce.2
